TPU v7x, 32 devices: a whole 2x2x4 slice. The times are simulated.
32 devices in a mesh: pb: 8 (over y, x, core), row: 4 (over z).
Axes of the slice: x: 2, y: 2, z: 4, core: 2. Of those that a mesh axis runs over, the one named last changes fastest.
Arguments:
- screened: bfloat16 [16, 2, 1024, 1024], P('pb', None, 'row'), may hold values from -1.0546875 to 1.0546875
- response: bfloat16 [16, 2, 1024, 1024], P(None, None, 'pb', 'row'), may hold values from -0.1875 to 0.1875
- q_owner: int32 [16], replicated, may hold values from 0 to 15, each once
- g_index: int32 [16, 1024], P('pb'), may hold values from 0 to 1023, each once within a row
Outputs:
- tangent: float32 [16, 2, 1024, 1024], P(None, None, ('row', 'pb'))
Inputs may be any that keep to these rules, and one draw needn't show every extreme that they name: `q_owner`: each owner slot appears once. `g_index`: each row is a permutation of the 1024 plane waves.
All inputs are finite; a program needn't handle non-finite values.
Results may differ from a plain program's by a relative error of at most 0.0029.
Values may be sent and summed in bfloat16 or wider, within the bound.
A program may use at most 64 MiB of HBM per device.

v0:
```python
import jax
import jax.numpy as jnp
from jax import lax
from jax.sharding import PartitionSpec as P


def complex_product(left, right):

    def product(first, second):
        return jnp.einsum("qik,qkj->qij", first, second, preferred_element_type=jnp.float32)

    real_part = product(left[:, 0], right[:, 0]) - product(left[:, 1], right[:, 1])
    imag_part = product(left[:, 0], right[:, 1]) + product(left[:, 1], right[:, 0])
    return jnp.stack((real_part, imag_part), axis=1)


def body(screened, response, q_owner, g_index):
    slot_count = q_owner.shape[0]
    inverse = (
        jnp.zeros((slot_count,), jnp.int32).at[q_owner].set(jnp.arange(slot_count, dtype=jnp.int32))
    )
    ordered = jnp.take(response, inverse, axis=0)
    at_owner = lax.all_to_all(ordered, "pb", split_axis=0, concat_axis=2, tiled=True)
    permuted = jax.vmap(lambda block, table: block[:, table, :])(at_owner, g_index)
    whole = lax.all_gather(screened, "row", axis=2, tiled=True)
    column_half = complex_product(whole, permuted).astype(jnp.bfloat16)
    halfway = lax.all_to_all(column_half, "row", split_axis=2, concat_axis=3, tiled=True)
    result = complex_product(halfway, whole)
    returned = lax.all_to_all(result, "pb", split_axis=2, concat_axis=0, tiled=True)
    return jnp.take(returned, q_owner, axis=0)


def solution(mesh):
    return jax.shard_map(
        body,
        mesh=mesh,
        in_specs=(P("pb", None, "row", None), P(None, None, "pb", "row"), P(), P("pb", None)),
        out_specs=P(None, None, ("row", "pb"), None),
        check_vma=False,
    )
```

profile of v0, /device:TPU:0, one launch (start us, length us, event | category | flops | bytes accessed | tf_op | source)
XLA Modules:
  0.0 326.9 jit_solution(15050981554449693041)
XLA Ops:
  6.5 0.0 copy-start
  6.5 0.0 all-gather.2.cloned.1.call-start
  6.5 3.2 copy.32
  9.8 0.0 copy-start.4
  9.8 0.0 all-gather.2.cloned.1.call-update
  9.8 0.6 copy-done.4
  10.4 0.6 scatter_custom_fusion
  11.1 0.0 copy-done
  11.1 2.0 gather_fusion
  13.1 3.2 broadcast_select_fusion.1
  16.3 0.0 copy-start.3
  16.3 5.3 %all-to-all-start = ((bf16[16,2,128,256]{3,2,1,0:T(8,128)(2,1)}), bf16[16,2,128,256]{3,2,1,0:T(8,128)(2,1)}, u32[]{:S(2)}, u32[]{:S(2)}) async-start(bf16[16,2,128,256]{3,2,1,0:T(8,128)(2,1)} %broadcast_select_fusion.1), calls=%async_computation | async-start | bytes 4194304 | tf_op jit(solution)/shard_map/all_to_all | solution.py:23
  21.6 0.0 copy-done.3
  21.7 26.7 %all-to-all-done = bf16[16,2,128,256]{3,2,1,0:T(8,128)(2,1)} async-done(((bf16[16,2,128,256]{3,2,1,0:T(8,128)(2,1)}), bf16[16,2,128,256]{3,2,1,0:T(8,128)(2,1)}, u32[]{:S(2)}, u32[]{:S(2)}) %all-to-all-start) | async-done | bytes 2097184 | tf_op jit(solution)/shard_map/all_to_all | solution.py:23
  48.3 1.7 copy.28
  50.1 3.5 %copy.29 = bf16[2,2,1024,256]{3,1,2,0:T(2,128)(2,1)} copy(bf16[2,2,1024,256]{3,2,1,0:T(8,128)(2,1)S(1)} %bitcast.86) | data formatting | bytes 4194304 | tf_op jit(solution)/shard_map/all_to_all | solution.py:23
  53.6 20.5 %gather_fusion.2 = bf16[2048,2,256]{2,1,0:T(2,128)(2,1)} fusion(bf16[2,2,1024,256]{3,1,2,0:T(2,128)(2,1)} %copy.29, s32[2048]{0:T(1024)S(1)} %bitcast.80), kind=kCustom, calls=%fused_computation.2 | custom fusion | bytes 4210688 | tf_op jit(solution)/shard_map/vmap()/gather | solution.py:24
  74.1 4.7 %copy.31 = bf16[2,1024,2,256]{1,3,0,2:T(8,128)(2,1)S(1)} copy(bf16[2,1024,2,256]{3,2,1,0:T(2,128)(2,1)} %bitcast.85) | data formatting | bytes 4194304 | tf_op jit(solution)/shard_map/vmap()/gather | solution.py:24
  78.8 83.5 %all-gather.2.cloned.1.call-done = bf16[2,2,1024,1024]{3,2,0,1:T(8,128)(2,1)} async-done(((bf16[2,2,256,1024]{3,2,0,1:T(8,128)(2,1)}), bf16[2,2,1024,1024]{3,2,0,1:T(8,128)(2,1)}) %all-gather.2.cloned.1.call-update) | async-done | bytes 8388624 | tf_op jit(solution)/shard_map/all_gather | solution.py:25
  162.3 0.0 copy-start.2
  162.3 3.6 %fusion.3 = f32[2,256,1024]{2,1,0:T(8,128)S(1)} fusion(bf16[2,2,1024,1024]{3,2,0,1:T(8,128)(2,1)} %all-gather.2.cloned.1.call-done, bf16[2,2,1024,256]{2,3,0,1:T(8,128)(2,1)S(1)} %bitcast.89), kind=kOutput, calls=%fused_computation.10 | convolution fusion | flops 1073741824 | bytes 7340032 | tf_op jit(solution)/shard_map/qik,qkj->qij/dot_general | solution.py:10
  165.9 1.0 copy-done.2
  166.9 1.4 fusion.2
  168.3 1.4 fusion.8
  169.8 1.4 fusion.9
  171.2 0.2 pad_maximum_fusion.1
  171.4 4.0 %copy.33 = bf16[2,2,1024,256]{3,0,1,2:T(2,128)(2,1)} copy(bf16[2,2,1024,256]{2,3,0,1:T(8,128)(2,1)S(1)} %pad_maximum_fusion.1) | data formatting | bytes 4194304 | tf_op jit(solution)/shard_map/stack | solution.py:14
  175.4 52.2 %all_to_all.54 = bf16[2,2,1024,256]{3,0,1,2:T(2,128)(2,1)S(1)} all-to-all(bf16[2,2,1024,256]{3,0,1,2:T(2,128)(2,1)} %copy.33), channel_id=1, replica_groups=mesh['pb'=8,'row'=4] {'row'}, dimensions={2} | all-to-all | bytes 4194304 | tf_op jit(solution)/shard_map/all_to_all | solution.py:27
  227.6 2.9 copy.43
  230.6 3.2 all_to_all.46
  233.8 0.0 slice-start
  233.8 3.6 %fusion.1 = f32[2,256,1024]{2,1,0:T(8,128)S(1)} fusion(bf16[2,2,1024,1024]{3,2,0,1:T(8,128)(2,1)} %all-gather.2.cloned.1.call-done, bf16[2,2,256,1024]{3,2,0,1:T(8,128)(2,1)S(1)} %all_to_all.46), kind=kOutput, calls=%fused_computation.8 | convolution fusion | flops 1073741824 | bytes 7340032 | tf_op jit(solution)/shard_map/qik,qkj->qij/dot_general | solution.py:10
  237.4 0.0 slice-start.1
  237.4 3.6 %fusion = f32[2,256,1024]{2,1,0:T(8,128)S(1)} fusion(bf16[2,2,1024,1024]{3,2,0,1:T(8,128)(2,1)} %all-gather.2.cloned.1.call-done, bf16[2,2,256,1024]{3,2,0,1:T(8,128)(2,1)S(1)} %all_to_all.46), kind=kOutput, calls=%fused_computation.7 | convolution fusion | flops 1073741824 | bytes 7340032 | tf_op jit(solution)/shard_map/qik,qkj->qij/dot_general | solution.py:10
  241.0 0.0 slice-done
  241.0 0.0 slice-done.1
  241.1 1.3 subtract_bitcast_fusion
  242.4 1.3 add_bitcast_fusion
  243.7 0.3 pad_maximum_fusion
  244.0 5.2 %copy.35 = f32[2,2,256,1024]{3,0,1,2:T(2,128)} copy(f32[2,2,256,1024]{3,2,0,1:T(8,128)S(1)} %pad_maximum_fusion) | data formatting | bytes 8388608 | tf_op jit(solution)/shard_map/stack | solution.py:14
  249.3 4.8 %all-to-all-start.2 = ((f32[2,2,256,1024]{3,0,1,2:T(2,128)}), f32[2,2,256,1024]{3,0,1,2:T(2,128)}, u32[]{:S(2)}, u32[]{:S(2)}) async-start(f32[2,2,256,1024]{3,0,1,2:T(2,128)} %copy.35), calls=%async_computation.2 | async-start | bytes 8388608 | tf_op jit(solution)/shard_map/all_to_all | solution.py:29
  254.1 48.8 %all-to-all-done.2 = f32[2,2,256,1024]{3,0,1,2:T(2,128)} async-done(((f32[2,2,256,1024]{3,0,1,2:T(2,128)}), f32[2,2,256,1024]{3,0,1,2:T(2,128)}, u32[]{:S(2)}, u32[]{:S(2)}) %all-to-all-start.2) | async-done | bytes 4194336 | tf_op jit(solution)/shard_map/all_to_all | solution.py:29
  302.9 4.6 %copy.36 = f32[2,2,256,1024]{3,2,1,0:T(8,128)S(1)} copy(f32[2,2,256,1024]{3,0,1,2:T(2,128)} %all-to-all-done.2) | data formatting | bytes 8388608 | tf_op jit(solution)/shard_map/all_to_all | solution.py:29
  307.5 2.3 copy.37
  309.9 4.9 %gather_fusion.1 = f32[16,2,32,1024]{3,2,1,0:T(8,128)} fusion(f32[16,2,32,1024]{3,2,1,0:T(8,128)} %bitcast.81, s32[1024]{0:T(1024)S(1)} %pad_clamp_fusion), kind=kCustom, calls=%fused_computation.1 | custom fusion | bytes 8388672 | tf_op jit(solution)/shard_map/jit(_take)/gather | solution.py:30
  314.8 0.0 copy-start.1
  314.8 5.3 %broadcast_select_fusion = f32[16,2,32,1024]{3,2,1,0:T(8,128)} fusion(f32[16,2,32,1024]{3,2,1,0:T(8,128)} %gather_fusion.1, pred[16]{0:T(512)(128)(4,1)S(1)} %compare_and_fusion.1), kind=kLoop, calls=%fused_computation.17 | loop fusion | flops 1048576 | bytes 8388624 | tf_op jit(solution)/shard_map/jit(_take)/select_n | solution.py:30
  320.1 0.0 copy-done.1
  (10 shorter events, 0.1 us)
Async XLA Ops:
  6.5 4.6 %copy-start = (bf16[16,2,128,256]{3,2,1,0:T(8,128)(2,1)S(1)}, bf16[16,2,128,256]{3,2,1,0:T(8,128)(2,1)}, u32[]{:S(2)}) copy-start(bf16[16,2,128,256]{3,2,1,0:T(8,128)(2,1)} %param.5) | copy-start | bytes 6291460
  6.5 155.7 %all-gather.2.cloned.1.call-start = ((), (), s32[]{:S(2)}) async-start(), calls=%async_computation.3 | async-start | bytes 10485760 | tf_op jit(solution)/shard_map/all_gather | solution.py:25
  9.8 0.7 copy-start.4
  16.3 5.3 %copy-start.3 = (s32[2,1024]{1,0:T(2,128)S(1)}, s32[2,1024]{1,0:T(2,128)}, u32[]{:S(2)}) copy-start(s32[2,1024]{1,0:T(2,128)} %param.7) | copy-start | bytes 24580
  16.3 32.0 %all-to-all-start = ((bf16[16,2,128,256]{3,2,1,0:T(8,128)(2,1)}), bf16[16,2,128,256]{3,2,1,0:T(8,128)(2,1)}, u32[]{:S(2)}, u32[]{:S(2)}) async-start(bf16[16,2,128,256]{3,2,1,0:T(8,128)(2,1)} %broadcast_select_fusion.1), calls=%async_computation | async-start | bytes 4194304 | tf_op jit(solution)/shard_map/all_to_all | solution.py:23
  162.3 4.6 %copy-start.2 = (bf16[2,2,1024,1024]{3,2,0,1:T(8,128)(2,1)S(1)}, bf16[2,2,1024,1024]{3,2,0,1:T(8,128)(2,1)}, u32[]{:S(2)}) copy-start(bf16[2,2,1024,1024]{3,2,0,1:T(8,128)(2,1)} %all-gather.2.cloned.1.call-done) | copy-start | bytes 25165828
  233.8 7.2 %slice-start = ((s8[8388608]{0:T(1024)(128)(4,1)}), s8[4194304]{0:T(1024)(128)(4,1)S(1)}, s32[]{:S(2)}) async-start(s8[8388608]{0:T(1024)(128)(4,1)} %bitcast.83), calls=%async_computation.4 | async-start | bytes 8388608
  237.4 3.6 %slice-start.1 = ((s8[8388608]{0:T(1024)(128)(4,1)}), s8[4194304]{0:T(1024)(128)(4,1)S(1)}, s32[]{:S(2)}) async-start(s8[8388608]{0:T(1024)(128)(4,1)} %bitcast.83), calls=%async_computation.5 | async-start | bytes 8388608
  249.3 53.7 %all-to-all-start.2 = ((f32[2,2,256,1024]{3,0,1,2:T(2,128)}), f32[2,2,256,1024]{3,0,1,2:T(2,128)}, u32[]{:S(2)}, u32[]{:S(2)}) async-start(f32[2,2,256,1024]{3,0,1,2:T(2,128)} %copy.35), calls=%async_computation.2 | async-start | bytes 8388608 | tf_op jit(solution)/shard_map/all_to_all | solution.py:29
  314.8 5.3 %copy-start.1 = (bf16[16,2,128,256]{3,2,1,0:T(8,128)(2,1)S(1)}, bf16[16,2,128,256]{3,2,1,0:T(8,128)(2,1)}, u32[]{:S(2)}) copy-start(bf16[16,2,128,256]{3,2,1,0:T(8,128)(2,1)} %param.5) | copy-start | bytes 6291460
Sparse Core Ops, SparseCore 0:
  9.9 152.3 all-gather.1
where the time goes:
time: 328 us; the launch traced here: 327 us
  waiting for transfers between devices  159 us (48%)
  local copies, waits for them, and re-layouts  65.4 us (20%)
  blocking collectives  52.2 us (16%)
  matrix products  17.6 us (5%)
  between operations  13.6 us (4%)
  starting transfers between devices  10.1 us (3%)
  other arithmetic  9.02 us (3%)
    all_gather x1, waiting for transfers between devices, body(): whole = lax.all_gather(screened, 'row', axis=2, tiled=True)  83.5 us
    all_to_all x1, blocking collectives, body(): lax.all_to_all(column_half, 'row', split_axis=2, concat_axis=3, tiled=True)  52.2 us
    all_to_all x1, waiting for transfers between devices, body(): lax.all_to_all(result, 'pb', split_axis=2, concat_axis=0, tiled=True)  48.8 us
    all_to_all x1, waiting for transfers between devices, body(): lax.all_to_all(ordered, 'pb', split_axis=0, concat_axis=2, tiled=True)  26.7 us
    gather x2, local copies, waits for them, and re-layouts, body(): block[:, table, :]  25.2 us
    dot_general x8, matrix products, product(): jnp.einsum('qik,qkj->qij', first, second, preferred_element_type=jnp.floa...  17.6 us
    another operation x2, local copies, waits for them, and re-layouts, complex_product(): return jnp.stack((real_part, imag_part), axis=1)  9.3 us
    all_to_all x2, local copies, waits for them, and re-layouts, body(): lax.all_to_all(result, 'pb', split_axis=2, concat_axis=0, tiled=True)  6.94 us
  transfers between devices with their start and end apart: 3, of which 3 were waited for; matrix products, arithmetic and copies ran while one was open for 11% of the time, Pallas kernels for 0%

commit v1 on v0

--- a/solution.py
+++ b/solution.py
@@ -24,7 +24,12 @@
     permuted = jax.vmap(lambda block, table: block[:, table, :])(at_owner, g_index)
     whole = lax.all_gather(screened, "row", axis=2, tiled=True)
     column_half = complex_product(whole, permuted).astype(jnp.bfloat16)
-    halfway = lax.all_to_all(column_half, "row", split_axis=2, concat_axis=3, tiled=True)
+    halfway = jnp.concatenate(
+        lax.all_to_all(
+            jnp.stack(jnp.split(column_half, lax.axis_size("row"), axis=2)), "row", 0, 0
+        ),
+        axis=3,
+    )
     result = complex_product(halfway, whole)
     returned = lax.all_to_all(result, "pb", split_axis=2, concat_axis=0, tiled=True)
     return jnp.take(returned, q_owner, axis=0)

time: 328 us -> 312 us (0.951)
  local copies, waits for them, and re-layouts: 65.4 us -> 55.2 us
  matrix products: 17.6 us -> 13.2 us
    all_to_all x2 -> x0, local copies, waits for them, and re-layouts: 6.17 us -> none  [body(): lax.all_to_all(column_half, 'row', split_axis=2, concat_axis=3, tiled=True)]
    dot_general x8, matrix products: 17.6 us -> 13.2 us  [product(): jnp.einsum('qik,qkj->qij', first, second, preferred_element_type=jnp.floa...]
    another operation x2 -> x1, local copies, waits for them, and re-layouts: 9.3 us -> 5.25 us  [complex_product(): return jnp.stack((real_part, imag_part), axis=1)]
  transfers between devices with their start and end apart: 3 -> 3, of which waited for: 3 -> 3; matrix products, arithmetic and copies ran while one was open for 11% -> 12% of each run, Pallas kernels for 0% -> 0%
where the time goes in v1:
time: 312 us
  waiting for transfers between devices  159 us (51%)
  local copies, waits for them, and re-layouts  55.2 us (18%)
  blocking collectives  51.1 us (16%)
  between operations  13.6 us (4%)
  matrix products  13.2 us (4%)
  starting transfers between devices  10.1 us (3%)
  other arithmetic  9.29 us (3%)
    all_gather x1, waiting for transfers between devices, body(): whole = lax.all_gather(screened, 'row', axis=2, tiled=True)  83.6 us
    all_to_all x1, blocking collectives, body(): lax.all_to_all(jnp.stack(jnp.split(column_half, lax.axis_size('row'), axi...  51.1 us
    all_to_all x1, waiting for transfers between devices, body(): lax.all_to_all(result, 'pb', split_axis=2, concat_axis=0, tiled=True)  48.8 us
    all_to_all x1, waiting for transfers between devices, body(): lax.all_to_all(ordered, 'pb', split_axis=0, concat_axis=2, tiled=True)  26.7 us
    gather x2, local copies, waits for them, and re-layouts, body(): block[:, table, :]  25.1 us
    dot_general x8, matrix products, product(): jnp.einsum('qik,qkj->qij', first, second, preferred_element_type=jnp.floa...  13.2 us
    all_to_all x2, local copies, waits for them, and re-layouts, body(): lax.all_to_all(result, 'pb', split_axis=2, concat_axis=0, tiled=True)  6.94 us
  transfers between devices with their start and end apart: 3, of which 3 were waited for; matrix products, arithmetic and copies ran while one was open for 12% of the time, Pallas kernels for 0%

profile of v1, /device:TPU:0, one launch (start us, length us, event | category | flops | bytes accessed | tf_op | source)
XLA Modules:
  0.0 311.5 jit_solution(4930561816397734482)
XLA Ops:
  6.5 0.0 copy-start
  6.5 0.0 all-gather.2.cloned.1.call-start
  6.5 3.2 %copy.36 = bf16[2,2,256,1024]{3,2,0,1:T(8,128)(2,1)} copy(bf16[2,2,256,1024]{3,2,1,0:T(8,128)(2,1)} %param.4) | data formatting | bytes 4194304 | tf_op args[0]
  9.8 0.0 copy-start.4
  9.8 0.0 all-gather.2.cloned.1.call-update
  9.8 0.6 copy-done.4
  10.4 0.6 scatter_custom_fusion
  11.1 0.0 copy-done
  11.1 2.0 gather_fusion
  13.1 3.2 %broadcast_select_fusion.1 = bf16[16,2,128,256]{3,2,1,0:T(8,128)(2,1)} fusion(bf16[16,2,128,256]{3,2,1,0:T(8,128)(2,1)} %gather_fusion, pred[16]{0:T(512)(128)(4,1)S(1)} %compare_and_fusion), kind=kLoop, calls=%fused_computation.27 | loop fusion | flops 1048576 | bytes 4194320 | tf_op jit(solution)/shard_map/jit(_take)/select_n | solution.py:22
  16.3 0.0 copy-start.3
  16.3 5.3 %all-to-all-start = ((bf16[16,2,128,256]{3,2,1,0:T(8,128)(2,1)}), bf16[16,2,128,256]{3,2,1,0:T(8,128)(2,1)}, u32[]{:S(2)}, u32[]{:S(2)}) async-start(bf16[16,2,128,256]{3,2,1,0:T(8,128)(2,1)} %broadcast_select_fusion.1), calls=%async_computation | async-start | bytes 4194304 | tf_op jit(solution)/shard_map/all_to_all | solution.py:23
  21.6 0.0 copy-done.3
  21.7 26.7 %all-to-all-done = bf16[16,2,128,256]{3,2,1,0:T(8,128)(2,1)} async-done(((bf16[16,2,128,256]{3,2,1,0:T(8,128)(2,1)}), bf16[16,2,128,256]{3,2,1,0:T(8,128)(2,1)}, u32[]{:S(2)}, u32[]{:S(2)}) %all-to-all-start) | async-done | bytes 2097184 | tf_op jit(solution)/shard_map/all_to_all | solution.py:23
  48.3 1.7 copy.32
  50.1 3.5 %copy.33 = bf16[2,2,1024,256]{3,1,2,0:T(2,128)(2,1)} copy(bf16[2,2,1024,256]{3,2,1,0:T(8,128)(2,1)S(1)} %bitcast.96) | data formatting | bytes 4194304 | tf_op jit(solution)/shard_map/all_to_all | solution.py:23
  53.6 20.4 %gather_fusion.2 = bf16[2048,2,256]{2,1,0:T(2,128)(2,1)} fusion(bf16[2,2,1024,256]{3,1,2,0:T(2,128)(2,1)} %copy.33, s32[2048]{0:T(1024)S(1)} %bitcast.88), kind=kCustom, calls=%fused_computation.2 | custom fusion | bytes 4210688 | tf_op jit(solution)/shard_map/vmap()/gather | solution.py:24
  74.0 4.7 %copy.35 = bf16[2,1024,2,256]{1,3,0,2:T(8,128)(2,1)S(1)} copy(bf16[2,1024,2,256]{3,2,1,0:T(2,128)(2,1)} %bitcast.95) | data formatting | bytes 4194304 | tf_op jit(solution)/shard_map/vmap()/gather | solution.py:24
  78.7 83.6 %all-gather.2.cloned.1.call-done = bf16[2,2,1024,1024]{3,2,0,1:T(8,128)(2,1)} async-done(((bf16[2,2,256,1024]{3,2,0,1:T(8,128)(2,1)}), bf16[2,2,1024,1024]{3,2,0,1:T(8,128)(2,1)}) %all-gather.2.cloned.1.call-update) | async-done | bytes 8388624 | tf_op jit(solution)/shard_map/all_gather | solution.py:25
  162.3 0.0 copy-start.2
  162.3 3.6 %fusion.2 = f32[2,256,1024]{2,1,0:T(8,128)S(1)} fusion(bf16[2,2,1024,1024]{3,2,0,1:T(8,128)(2,1)} %all-gather.2.cloned.1.call-done, bf16[2,2,1024,256]{2,3,0,1:T(8,128)(2,1)S(1)} %bitcast.98), kind=kOutput, calls=%fused_computation.9 | convolution fusion | flops 1073741824 | bytes 7340032 | tf_op jit(solution)/shard_map/qik,qkj->qij/dot_general | solution.py:10
  165.9 1.0 copy-done.2
  166.9 1.4 fusion.3
  168.3 1.4 fusion.9
  169.8 1.4 fusion.8
  171.2 0.2 fusion.13
  171.4 0.3 pad_maximum_fusion.1
  171.7 51.1 %all_to_all.41 = bf16[4,2,2,256,256]{3,4,1,2,0:T(8,128)(2,1)S(1)} all-to-all(bf16[4,2,2,256,256]{3,4,1,2,0:T(8,128)(2,1)S(1)} %pad_maximum_fusion.1), channel_id=1, replica_groups=mesh['pb'=8,'row'=4] {'row'}, dimensions={0} | all-to-all | bytes 4194304 | tf_op jit(solution)/shard_map/all_to_all | solution.py:28
  222.8 0.1 copy.37
  222.9 1.3 fusion.1
  224.2 1.3 fusion
  225.6 1.3 subtract_bitcast_fusion
  226.9 1.3 add_bitcast_fusion
  228.3 0.3 pad_maximum_fusion
  228.6 5.2 %copy.40 = f32[2,2,256,1024]{3,0,1,2:T(2,128)} copy(f32[2,2,256,1024]{3,2,0,1:T(8,128)S(1)} %pad_maximum_fusion) | data formatting | bytes 8388608 | tf_op jit(solution)/shard_map/stack | solution.py:14
  233.8 4.8 %all-to-all-start.2 = ((f32[2,2,256,1024]{3,0,1,2:T(2,128)}), f32[2,2,256,1024]{3,0,1,2:T(2,128)}, u32[]{:S(2)}, u32[]{:S(2)}) async-start(f32[2,2,256,1024]{3,0,1,2:T(2,128)} %copy.40), calls=%async_computation.2 | async-start | bytes 8388608 | tf_op jit(solution)/shard_map/all_to_all | solution.py:34
  238.6 48.8 %all-to-all-done.2 = f32[2,2,256,1024]{3,0,1,2:T(2,128)} async-done(((f32[2,2,256,1024]{3,0,1,2:T(2,128)}), f32[2,2,256,1024]{3,0,1,2:T(2,128)}, u32[]{:S(2)}, u32[]{:S(2)}) %all-to-all-start.2) | async-done | bytes 4194336 | tf_op jit(solution)/shard_map/all_to_all | solution.py:34
  287.5 4.6 %copy.41 = f32[2,2,256,1024]{3,2,1,0:T(8,128)S(1)} copy(f32[2,2,256,1024]{3,0,1,2:T(2,128)} %all-to-all-done.2) | data formatting | bytes 8388608 | tf_op jit(solution)/shard_map/all_to_all | solution.py:34
  292.1 2.3 copy.42
  294.4 5.0 %gather_fusion.1 = f32[16,2,32,1024]{3,2,1,0:T(8,128)} fusion(f32[16,2,32,1024]{3,2,1,0:T(8,128)} %bitcast.89, s32[1024]{0:T(1024)S(1)} %pad_clamp_fusion), kind=kCustom, calls=%fused_computation.1 | custom fusion | bytes 8388672 | tf_op jit(solution)/shard_map/jit(_take)/gather | solution.py:35
  299.4 0.0 copy-start.1
  299.4 5.3 %broadcast_select_fusion = f32[16,2,32,1024]{3,2,1,0:T(8,128)} fusion(f32[16,2,32,1024]{3,2,1,0:T(8,128)} %gather_fusion.1, pred[16]{0:T(512)(128)(4,1)S(1)} %compare_and_fusion.1), kind=kLoop, calls=%fused_computation.22 | loop fusion | flops 1048576 | bytes 8388624 | tf_op jit(solution)/shard_map/jit(_take)/select_n | solution.py:35
  304.7 0.0 copy-done.1
  (9 shorter events, 0.1 us)
Async XLA Ops:
  6.5 4.6 %copy-start = (bf16[16,2,128,256]{3,2,1,0:T(8,128)(2,1)S(1)}, bf16[16,2,128,256]{3,2,1,0:T(8,128)(2,1)}, u32[]{:S(2)}) copy-start(bf16[16,2,128,256]{3,2,1,0:T(8,128)(2,1)} %param.5) | copy-start | bytes 6291460
  6.5 155.7 %all-gather.2.cloned.1.call-start = ((), (), s32[]{:S(2)}) async-start(), calls=%async_computation.3 | async-start | bytes 10485760 | tf_op jit(solution)/shard_map/all_gather | solution.py:25
  9.8 0.7 copy-start.4
  16.3 5.3 %copy-start.3 = (s32[2,1024]{1,0:T(2,128)S(1)}, s32[2,1024]{1,0:T(2,128)}, u32[]{:S(2)}) copy-start(s32[2,1024]{1,0:T(2,128)} %param.7) | copy-start | bytes 24580
  16.3 32.0 %all-to-all-start = ((bf16[16,2,128,256]{3,2,1,0:T(8,128)(2,1)}), bf16[16,2,128,256]{3,2,1,0:T(8,128)(2,1)}, u32[]{:S(2)}, u32[]{:S(2)}) async-start(bf16[16,2,128,256]{3,2,1,0:T(8,128)(2,1)} %broadcast_select_fusion.1), calls=%async_computation | async-start | bytes 4194304 | tf_op jit(solution)/shard_map/all_to_all | solution.py:23
  162.3 4.6 %copy-start.2 = (bf16[2,2,1024,1024]{3,2,0,1:T(8,128)(2,1)S(1)}, bf16[2,2,1024,1024]{3,2,0,1:T(8,128)(2,1)}, u32[]{:S(2)}) copy-start(bf16[2,2,1024,1024]{3,2,0,1:T(8,128)(2,1)} %all-gather.2.cloned.1.call-done) | copy-start | bytes 25165828
  233.8 53.6 %all-to-all-start.2 = ((f32[2,2,256,1024]{3,0,1,2:T(2,128)}), f32[2,2,256,1024]{3,0,1,2:T(2,128)}, u32[]{:S(2)}, u32[]{:S(2)}) async-start(f32[2,2,256,1024]{3,0,1,2:T(2,128)} %copy.40), calls=%async_computation.2 | async-start | bytes 8388608 | tf_op jit(solution)/shard_map/all_to_all | solution.py:34
  299.4 5.3 %copy-start.1 = (bf16[16,2,128,256]{3,2,1,0:T(8,128)(2,1)S(1)}, bf16[16,2,128,256]{3,2,1,0:T(8,128)(2,1)}, u32[]{:S(2)}) copy-start(bf16[16,2,128,256]{3,2,1,0:T(8,128)(2,1)} %param.5) | copy-start | bytes 6291460
Sparse Core Ops, SparseCore 0:
  9.9 152.3 all-gather.1
